TPU v7x, 32 devices: a whole 2x2x4 slice. The times are simulated.
32 devices in a mesh: grp: 4 (over z), seq: 8 (over y, x, core).
Axes of the slice: x: 2, y: 2, z: 4, core: 2. Of those that a mesh axis runs over, the one named last changes fastest.
Arguments:
- tokens: bfloat16 [4096, 2048], P(('grp', 'seq')), may hold values from -6 to 6
- norm_gains: float32 [2, 2048], replicated, may hold values from 0.5 to 1.5
- norm_biases: float32 [2, 2048], replicated, may hold values from -1 to 1
- mix_weight: bfloat16 [2048, 3, 2048], P(None, None, 'seq'), may hold values from -0.125 to 0.125
- mix_bias: bfloat16 [3, 2048], P(None, 'seq'), may hold values from -1.796875 to 1.796875
- out_weight: bfloat16 [2048, 2048], P('seq'), may hold values from -0.5 to 0.5
- gate_up_weight: bfloat16 [2048, 2, 5632], P(None, None, 'seq'), may hold values from -0.125 to 0.125
- down_weight: bfloat16 [5632, 2048], P('seq'), may hold values from -0.078125 to 0.078125
- row_lengths: int32 [8], replicated, may hold values from 128 to 1024, as said below
- row_group: int32 [8], replicated, may hold values from 0 to 3, as said below
- cotangent: bfloat16 [4096, 2048], P(('grp', 'seq')), may hold values from -6 to 6
Outputs:
- layer_out: bfloat16 [4096, 2048], P(('grp', 'seq'))
- tokens_grad: bfloat16 [4096, 2048], P(('grp', 'seq'))
- gains_grad: float32 [2, 2048], replicated
- biases_grad: float32 [2, 2048], replicated
- mix_grad: float32 [2048, 3, 2048], P(None, None, 'seq')
- mix_bias_grad: float32 [3, 2048], P(None, 'seq')
- out_grad: float32 [2048, 2048], P('seq')
- gate_up_grad: float32 [2048, 2, 5632], P(None, None, 'seq')
- down_grad: float32 [5632, 2048], P('seq')
Inputs may be any that keep to these rules, and one draw needn't show every extreme that they name: `row_lengths`: rows 0 to 1 are 1024 long; every other row's length is a multiple of 128 and at most 256. `row_group`: each of rows 0 to 1 fills a group alone; every other group holds exactly three of the other rows.
All inputs are finite; a program needn't handle non-finite values.
Results may differ from a plain program's by a relative error of at most 0.02.
Values may be sent and summed in bfloat16 or wider, within the bound.
A program may use at most 320 MiB of HBM per device.

v0:
```python
import math
import jax
import jax.numpy as jnp
from jax import lax
from jax.sharding import PartitionSpec as P

HEAD_DIM = 64
ROT = 16
EPS = 1e-05
NEG = -1e30
BASE = 10000.0


def layer_norm(values, gain, bias):
    centered = values - jnp.mean(values, axis=-1, keepdims=True)
    scale = lax.rsqrt(jnp.mean(centered * centered, axis=-1, keepdims=True) + EPS)
    unit = centered * scale
    return (unit * gain + bias, unit, scale)


def norm_back(incoming, unit, scale, gain):
    along = incoming * gain
    inner = jnp.mean(along, axis=-1, keepdims=True)
    cross = jnp.mean(along * unit, axis=-1, keepdims=True)
    return (
        scale * (along - inner - unit * cross),
        jnp.sum(incoming * unit, axis=0),
        jnp.sum(incoming, axis=0),
    )


def rotate(values, where, sign):
    half = ROT // 2
    freq = BASE ** (-jnp.arange(half, dtype=jnp.float32) / half)
    angle = where.astype(jnp.float32)[:, None] * freq[None, :]
    cosine = jnp.cos(angle)[:, None, :]
    sine = sign * jnp.sin(angle)[:, None, :]
    first = values[..., :half]
    second = values[..., half:ROT]
    return jnp.concatenate(
        [first * cosine - second * sine, second * cosine + first * sine, values[..., ROT:]], axis=-1
    )


def unrotate(lowered, where):
    wide = lowered.astype(jnp.float32)
    turned = jnp.stack(
        [rotate(wide[:, 0], where, -1.0), rotate(wide[:, 1], where, -1.0), wide[:, 2]], axis=1
    )
    return turned.reshape(lowered.shape[0], 3, -1).astype(jnp.bfloat16)


def slot_rows(row_lengths, row_group, group, slots):
    order = jnp.arange(row_lengths.shape[0], dtype=jnp.int32)
    same = row_group == group
    earlier = (order[:, None] > order[None, :]) & same[None, :]
    begin = jnp.sum(jnp.where(earlier, row_lengths[None, :], 0), axis=1)
    finish = begin + row_lengths
    inside = same[None, :] & (slots[:, None] >= begin[None, :]) & (slots[:, None] < finish[None, :])
    label = jnp.sum(jnp.where(inside, order[None, :] + 1, 0), axis=1) - 1
    offset = jnp.sum(jnp.where(inside, slots[:, None] - begin[None, :], 0), axis=1)
    load = jnp.sum(jnp.where(same, row_lengths, 0))
    return (label, jnp.where(label < 0, slots - load, offset))


def block_scores(query, key, label, start, block):
    part = lax.dynamic_slice_in_dim(query, start, block, 0)
    rows = start + jnp.arange(block, dtype=jnp.int32)
    columns = jnp.arange(label.shape[0], dtype=jnp.int32)
    label_rows = lax.dynamic_slice_in_dim(label, start, block, 0)
    allowed = (label_rows[:, None] == label[None, :]) & (rows[:, None] >= columns[None, :])
    scores = jnp.einsum("qhe,khe->hqk", part, key, preferred_element_type=jnp.float32) * (
        1.0 / math.sqrt(query.shape[-1])
    )
    return (part, jnp.where(allowed[None], scores, NEG))


def attend(query, key, value, label, block):

    def one_block(index):
        part, scores = block_scores(query, key, label, index * block, block)
        top = jnp.max(scores, axis=-1, keepdims=True)
        weights = jnp.exp(scores - top)
        totals = jnp.sum(weights, axis=-1, keepdims=True)
        probs = (weights / totals).astype(jnp.bfloat16)
        mixed = jnp.einsum("hqk,khe->qhe", probs, value, preferred_element_type=jnp.float32)
        return (mixed, top[..., 0] + jnp.log(totals[..., 0]))

    mixed, log_totals = lax.map(one_block, jnp.arange(query.shape[0] // block, dtype=jnp.int32))
    return (mixed.reshape(query.shape), log_totals)


def attend_back(query, key, value, label, log_totals, mixed_back, block):
    scale = 1.0 / math.sqrt(query.shape[-1])

    def one_block(carry, index):
        key_back, value_back = carry
        start = index * block
        part, scores = block_scores(query, key, label, start, block)
        back_part = lax.dynamic_slice_in_dim(mixed_back, start, block, 0)
        probs = jnp.exp(scores - log_totals[index][..., None])
        value_back = value_back + jnp.einsum(
            "hqk,qhe->khe",
            probs.astype(jnp.bfloat16),
            back_part,
            preferred_element_type=jnp.float32,
        )
        probs_back = jnp.einsum(
            "qhe,khe->hqk", back_part, value, preferred_element_type=jnp.float32
        )
        inner = jnp.sum(probs_back * probs, axis=-1, keepdims=True)
        score_back = (probs * (probs_back - inner)).astype(jnp.bfloat16)
        query_back = (
            jnp.einsum("hqk,khe->qhe", score_back, key, preferred_element_type=jnp.float32) * scale
        )
        key_back = (
            key_back
            + jnp.einsum("hqk,qhe->khe", score_back, part, preferred_element_type=jnp.float32)
            * scale
        )
        return ((key_back, value_back), query_back)

    empty = jnp.zeros(key.shape, jnp.float32)
    (key_back, value_back), query_back = lax.scan(
        one_block, (empty, empty), jnp.arange(query.shape[0] // block, dtype=jnp.int32)
    )
    return (query_back.reshape(query.shape), key_back, value_back)


def silu_parts(gate_up):
    gate = gate_up[:, 0]
    upper = gate_up[:, 1]
    sigma = jax.nn.sigmoid(gate)
    return (gate * sigma * upper, gate, upper, sigma)


def gate_back(hidden_back, gate, upper, sigma):
    gate_part = hidden_back * upper * sigma * (1.0 + gate * (1.0 - sigma))
    up_part = hidden_back * gate * sigma
    return jnp.stack([gate_part, up_part], axis=1).astype(jnp.bfloat16)


def gather_rows(values):
    return lax.all_gather(values, "seq", axis=0, tiled=True)


def summed_rows(product, left):
    return lax.psum_scatter(
        product(left).astype(jnp.bfloat16), "seq", scatter_dimension=0, tiled=True
    ).astype(jnp.float32)


def on_device(
    tokens,
    norm_gains,
    norm_biases,
    mix_weight,
    mix_bias,
    out_weight,
    gate_up_weight,
    down_weight,
    row_lengths,
    row_group,
    cotangent,
):
    seq_count = lax.axis_size("seq")
    shard = lax.axis_index("seq")
    group = lax.axis_index("grp")
    slots_dev = tokens.shape[0]
    width = tokens.shape[1]
    group_slots = slots_dev * seq_count
    block = min(512, group_slots)
    local_width = width // seq_count
    local_heads = local_width // HEAD_DIM
    mine = shard * slots_dev + jnp.arange(slots_dev, dtype=jnp.int32)
    label_mine, place_mine = slot_rows(row_lengths, row_group, group, mine)
    label_all, place_all = slot_rows(
        row_lengths, row_group, group, jnp.arange(group_slots, dtype=jnp.int32)
    )
    inputs = tokens.astype(jnp.float32)
    upstream = cotangent.astype(jnp.float32) * (label_mine >= 0).astype(jnp.float32)[:, None]
    upstream_low = upstream.astype(jnp.bfloat16)
    normed, unit_one, scale_one = layer_norm(inputs, norm_gains[0], norm_biases[0])
    normed_low = normed.astype(jnp.bfloat16)
    mix_full, bias_full, out_full = (
        lax.all_gather(mix_weight, "seq", axis=2, tiled=True),
        lax.all_gather(mix_bias, "seq", axis=1, tiled=True),
        lax.all_gather(out_weight, "seq", axis=0, tiled=True),
    )
    mixin = jnp.einsum(
        "td,dcf->tcf", normed_low, mix_full, preferred_element_type=jnp.float32
    ) + bias_full.astype(jnp.float32)
    heads_in = mixin.reshape(slots_dev, 3, width // HEAD_DIM, HEAD_DIM)
    sending = jnp.stack(
        [
            rotate(heads_in[:, 0], place_mine, 1.0),
            rotate(heads_in[:, 1], place_mine, 1.0),
            heads_in[:, 2],
        ],
        axis=1,
    ).astype(jnp.bfloat16)
    arrived = lax.all_to_all(
        sending.reshape(slots_dev, 3, seq_count, local_width),
        "seq",
        split_axis=2,
        concat_axis=0,
        tiled=True,
    )
    arrived = arrived.reshape(group_slots, 3, local_heads, HEAD_DIM)
    query, key, value = (arrived[:, 0], arrived[:, 1], arrived[:, 2])
    mixed, log_totals = attend(query, key, value, label_all, block)
    attended = lax.all_to_all(
        mixed.reshape(group_slots, local_width).astype(jnp.bfloat16),
        "seq",
        split_axis=0,
        concat_axis=1,
        tiled=True,
    )
    resid = inputs + jnp.dot(attended, out_full, preferred_element_type=jnp.float32)
    normed_two, unit_two, scale_two = layer_norm(resid, norm_gains[1], norm_biases[1])
    normed_two_all = gather_rows(normed_two.astype(jnp.bfloat16))
    gate_up = jnp.einsum(
        "td,dcf->tcf", normed_two_all, gate_up_weight, preferred_element_type=jnp.float32
    )
    hidden, gate, upper, sigma = silu_parts(gate_up)
    hidden_low = hidden.astype(jnp.bfloat16)

    def down_product(part):
        return jnp.dot(part, down_weight, preferred_element_type=jnp.float32)

    layer_out = resid + summed_rows(down_product, hidden_low)
    upstream_all = gather_rows(upstream_low)
    down_shard = jnp.einsum(
        "tf,td->fd", hidden_low, upstream_all, preferred_element_type=jnp.float32
    )
    hidden_back = jnp.einsum(
        "td,fd->tf", upstream_all, down_weight, preferred_element_type=jnp.float32
    )
    gate_up_back = gate_back(hidden_back, gate, upper, sigma)
    gate_up_shard = jnp.einsum(
        "td,tcf->dcf", normed_two_all, gate_up_back, preferred_element_type=jnp.float32
    )

    def gate_up_product(part):
        return jnp.einsum("tcf,dcf->td", part, gate_up_weight, preferred_element_type=jnp.float32)

    normed_two_back = summed_rows(gate_up_product, gate_up_back)
    resid_part, gain_two, bias_two = norm_back(normed_two_back, unit_two, scale_two, norm_gains[1])
    resid_back = upstream + resid_part
    branch_low = resid_back.astype(jnp.bfloat16)
    out_term = jnp.einsum("te,td->ed", attended, branch_low, preferred_element_type=jnp.float32)
    attended_back = jnp.einsum(
        "td,ed->te", branch_low, out_full, preferred_element_type=jnp.float32
    ).astype(jnp.bfloat16)
    heads_back = lax.all_to_all(
        attended_back, "seq", split_axis=1, concat_axis=0, tiled=True
    ).reshape(group_slots, local_heads, HEAD_DIM)
    query_back, key_back, value_back = attend_back(
        query, key, value, label_all, log_totals, heads_back, block
    )
    lowered = (
        jnp.stack([query_back, key_back, value_back], axis=1)
        .astype(jnp.bfloat16)
        .reshape(group_slots, 3, 1, local_width)
    )
    returned = lax.all_to_all(lowered, "seq", split_axis=0, concat_axis=2, tiled=True).reshape(
        slots_dev, 3, width // HEAD_DIM, HEAD_DIM
    )
    mixin_back = unrotate(returned, place_mine)
    mix_term = jnp.einsum("td,tcf->dcf", normed_low, mixin_back, preferred_element_type=jnp.float32)
    bias_term = jnp.sum(mixin_back, axis=0, dtype=jnp.float32)
    normed_back = jnp.einsum(
        "tcf,dcf->td", mixin_back, mix_full, preferred_element_type=jnp.float32
    )
    mix_shard, bias_shard, out_shard = (
        lax.psum_scatter(
            mix_term.astype(jnp.bfloat16), "seq", scatter_dimension=2, tiled=True
        ).astype(jnp.float32),
        lax.psum_scatter(
            bias_term.astype(jnp.bfloat16), "seq", scatter_dimension=1, tiled=True
        ).astype(jnp.float32),
        lax.psum_scatter(
            out_term.astype(jnp.bfloat16), "seq", scatter_dimension=0, tiled=True
        ).astype(jnp.float32),
    )
    tokens_part, gain_one, bias_one = norm_back(normed_back, unit_one, scale_one, norm_gains[0])
    tokens_grad = (resid_back + tokens_part).astype(jnp.bfloat16)
    mix_grad, mix_bias_grad, out_grad, gate_up_grad, down_grad = (
        lax.psum(mix_shard.astype(jnp.bfloat16), "grp").astype(jnp.float32),
        lax.psum(bias_shard.astype(jnp.bfloat16), "grp").astype(jnp.float32),
        lax.psum(out_shard.astype(jnp.bfloat16), "grp").astype(jnp.float32),
        lax.psum(gate_up_shard.astype(jnp.bfloat16), "grp").astype(jnp.float32),
        lax.psum(down_shard.astype(jnp.bfloat16), "grp").astype(jnp.float32),
    )
    gains_grad, biases_grad = lax.psum(
        (jnp.stack([gain_one, gain_two]), jnp.stack([bias_one, bias_two])), ("grp", "seq")
    )
    return (
        layer_out.astype(jnp.bfloat16),
        tokens_grad,
        gains_grad,
        biases_grad,
        mix_grad,
        mix_bias_grad,
        out_grad,
        gate_up_grad,
        down_grad,
    )


def solution(mesh):
    placed = (
        P(("grp", "seq"), None),
        P(),
        P(),
        P(None, None, "seq"),
        P(None, "seq"),
        P("seq", None),
        P(None, None, "seq"),
        P("seq", None),
        P(),
        P(),
        P(("grp", "seq"), None),
    )
    return jax.shard_map(
        on_device,
        mesh=mesh,
        in_specs=placed,
        out_specs=(
            P(("grp", "seq"), None),
            P(("grp", "seq"), None),
            P(),
            P(),
            P(None, None, "seq"),
            P(None, "seq"),
            P("seq", None),
            P(None, None, "seq"),
            P("seq", None),
        ),
        check_vma=False,
    )
```

profile of v0, /device:TPU:0, one launch (start us, length us, event | category | flops | bytes accessed | tf_op | source)
XLA Modules:
  0.0 1248.3 jit_solution(738130817734868844)
XLA Ops:
  9.5 10.4 all_gather.16
  21.9 121.0 %all-gather.5.cloned.1.call-done = bf16[2048,3,2048]{2,0,1:T(8,128)(2,1)} async-done(((bf16[2048,3,256]{2,0,1:T(8,128)(2,1)}), bf16[2048,3,2048]{2,0,1:T(8,128)(2,1)}) %all-gather.5.cloned.1.call-update) | async-done | bytes 25165840 | tf_op jit(solution)/shard_map/all_gather | solution.py:186
  143.0 13.4 %convolution_add_fusion = f32[128,3,2048]{2,0,1:T(8,128)} fusion(bf16[2048,3,2048]{2,0,1:T(8,128)(2,1)} %all-gather.5.cloned.1.call-done, f32[3,2048]{1,0:T(4,128)S(1)} %convert_element_type.139, bf16[128,2048]{1,0:T(8,128)(2,1)S(1)} %copy-done.5, f32[2048]{0:T(1024)S(1)} %bitcast.195, f32[2048]{0:T(1024)S(1)} %bitcast.191, f32[128]{0:T(128)S(1)} %add_rsqrt_fusion.1, ...), kind=kOutput, calls=%fused_computation.63 | convolution fusion | flops 3223584768 | bytes 28877824 | tf_op jit(solution)/shard_map/td,dcf->tcf/dot_general | solution.py:190
  156.4 3.5 copy.90
  164.7 4.5 all-to-all-start
  169.3 35.6 %all-to-all-done = bf16[128,3,8,256]{0,3,1,2:T(8,128)(2,1)} async-done(((bf16[128,3,8,256]{0,3,1,2:T(8,128)(2,1)}), bf16[128,3,8,256]{0,3,1,2:T(8,128)(2,1)}, u32[]{:S(2)}, u32[]{:S(2)}) %all-to-all-start) | async-done | bytes 1572896 | tf_op jit(solution)/shard_map/all_to_all | solution.py:202
  204.9 3.6 copy.92
  208.5 3.7 reshape.381
  212.2 2.6 slice_bitcast_fusion.6
  215.6 21.5 %while.27 = (s32[]{:T(128)}, bf16[2,512,4,64]{1,3,2,0:T(8,128)(2,1)}, f32[2,4,512]{2,1,0:T(4,128)S(1)}, s32[2]{0:T(128)S(1)}, s32[1024]{0:T(1024)S(1)}, /*index=...) while((s32[]{:T(128)}, ...), condition=%wide.region_10.11_spmd, body=%wide.region_7.10_spmd.sunk | while | flops 563608064 | bytes 35469596 | solution.py:89
  217.5 2.6 fusion.126
  222.5 3.0 fusion.128
  228.2 2.6 fusion.126
  233.3 3.0 fusion.128
  243.5 4.2 all-to-all-start.1
  247.8 9.7 all-to-all-done.1
  257.4 4.9 fusion.81
  266.9 33.4 %all-gather.9.cloned.1.call-done = bf16[1024,2048]{1,0:T(8,128)(2,1)} async-done(((bf16[128,2048]{1,0:T(8,128)(2,1)}), bf16[1024,2048]{1,0:T(8,128)(2,1)}) %all-gather.9.cloned.1.call-update) | async-done | bytes 4194320 | tf_op jit(solution)/shard_map/all_gather | solution.py:144
  300.4 11.0 fusion.39
  311.4 28.1 %all-gather.11.cloned.1.call-done = bf16[1024,2048]{1,0:T(8,128)(2,1)} async-done(((bf16[128,2048]{1,0:T(8,128)(2,1)}), bf16[1024,2048]{1,0:T(8,128)(2,1)}) %all-gather.11.cloned.1.call-update) | async-done | bytes 4194320 | tf_op jit(solution)/shard_map/all_gather | solution.py:144
  339.5 8.3 fusion.45
  349.4 11.0 bitcast_convert_fusion
  360.4 6.4 convolution_convert_fusion.3
  366.9 45.0 %reduce-scatter.10.cloned.1.call-done = bf16[128,2048]{1,0:T(8,128)(2,1)} async-done(((bf16[1024,2048]{1,0:T(8,128)(2,1)}), bf16[128,2048]{1,0:T(8,128)(2,1)}) %reduce-scatter.10.cloned.1.call-update) | async-done | bytes 524304 | tf_op jit(solution)/shard_map/reduce_scatter | solution.py:148
  414.0 53.4 %reduce-scatter.8.cloned.1.call-done = bf16[128,2048]{1,0:T(8,128)(2,1)} async-done(((bf16[1024,2048]{1,0:T(8,128)(2,1)}), bf16[128,2048]{1,0:T(8,128)(2,1)}) %reduce-scatter.8.cloned.1.call-update) | async-done | bytes 524304 | tf_op jit(solution)/shard_map/reduce_scatter | solution.py:148
  469.7 7.1 convolution_convert_fusion.1
  476.8 6.3 convolution_convert_fusion.5
  484.0 3.5 all-to-all-start.2
  487.7 9.4 all-to-all-done.2
  501.1 31.6 %while.28 = (s32[]{:T(128)}, f32[1024,4,64]{0,2,1:T(8,128)S(1)}, f32[1024,4,64]{0,2,1:T(8,128)}, bf16[2,512,4,64]{1,3,2,0:T(8,128)(2,1)}, s32[2]{0:T(128)S(1)}, ...) while((s32[]{:T(128)}, f32[1024,4,64]{0,2,1:T(8,128)S(1)}, ...), condition=%wide.region_19.20_spmd.clone, body=%wide.region_17.19_spmd.clone.sunk | while | flops 1376647680 | bytes 87103920 | solution.py:124
  506.4 2.5 fusion.141
  508.9 3.2 multiply_reduce_fusion.4
  522.2 2.6 fusion.141
  524.7 3.2 multiply_reduce_fusion.4
  537.6 3.0 copy.98
  540.5 29.5 %all_to_all.56 = bf16[1024,3,1,256]{3,1,2,0:T(4,128)(2,1)S(1)} all-to-all(bf16[1024,3,1,256]{3,1,2,0:T(4,128)(2,1)S(1)} %copy.98), channel_id=1, replica_groups=mesh['grp'=4,'seq'=8] {'seq'}, dimensions={0} | all-to-all | bytes 3145728 | tf_op jit(solution)/shard_map/all_to_all | solution.py:266
  578.5 12.0 convolution_convert_fusion
  590.6 10.8 convolution_convert_fusion.2
  603.1 8.9 convolution_convert_fusion.4
  612.0 134.7 %reduce-scatter.12.cloned.1.call-done = bf16[2048,3,256]{2,0,1:T(8,128)(2,1)} async-done(((bf16[2048,3,2048]{2,0,1:T(8,128)(2,1)}), bf16[2048,3,256]{2,0,1:T(8,128)(2,1)}) %reduce-scatter.12.cloned.1.call-update) | async-done | bytes 3145744 | tf_op jit(solution)/shard_map/reduce_scatter | solution.py:276
  746.7 14.6 %fusion.59 = (f32[2048]{0:T(1024)S(1)}, f32[128]{0:T(128)S(1)}, f32[128]{0:T(128)S(1)}, f32[2048]{0:T(1024)S(1)}, f32[128,2048]{1,0:T(8,128)}) fusion(bf16[128,2048]{1,0:T(8,128)(2,1)S(1)} %copy-done.6, f32[128]{0:T(128)S(1)} %copy-done.35, f32[128]{0:T(128)S(1)} %copy-done.33, f32[2048]{0:T(1024)S(1)} %bitcast.193, ...), kind=kOutput, calls=%fused_computation.93 | convolution fusion | flops 3225415680 | bytes 28338176 | tf_op jit(solution)/shard_map/tcf,dcf->td/dot_general | solution.py:272
  761.4 40.2 %all-reduce = (f32[2,2048]{1,0:T(2,128)}, f32[2,2048]{1,0:T(2,128)}) all-reduce(f32[2,2048]{1,0:T(2,128)S(1)} %pad_maximum_fusion.10, f32[2,2048]{1,0:T(2,128)S(1)} %pad_maximum_fusion.11), channel_id=1, replica_groups=mesh['grp'=4,'seq'=8] {'grp','seq'}, use_global_device_ids=true, to_apply=%region_24.25 | all-reduce | flops 8192 | bytes 65536 | tf_op jit(solution)/shard_map/psum | solution.py:295
  805.0 12.3 psum.52
  817.9 407.1 %all-reduce.4.cloned.1.call-done = (bf16[2048,3,256]{2,0,1:T(8,128)(2,1)}, bf16[256,2048]{1,0:T(8,128)(2,1)}, bf16[2048,2,704]{0,2,1:T(8,128)(2,1)}, bf16[704,2048]{1,0:T(8,128)(2,1)}) async-done(((bf16[2048,3,256]{2,0,1:T(8,128)(2,1)}, bf16[256,2048]{1,0:T(8,128)(2,1)}, bf16[2048,2,704]{0,2,1:T(8,128)(2,1)}, bf16[704,2048]{1,0:T(8,128)(2,1)}), (bf16[2048,3,256]{2,0,1:T(8,128)(2,1)}, ...) | async-done | bytes 12845072 | tf_op jit(solution)/shard_map/psum | solution.py:289
  1225.0 2.9 convert_element_type.164
  1228.0 3.7 convert_element_type.161
  1231.7 3.3 convert_element_type.168
  1235.0 6.0 convert_element_type.166
  (232 shorter events, 74.7 us)
Async XLA Ops:
  7.2 332.3 %copy-start = (bf16[704,2048]{1,0:T(8,128)(2,1)S(1)}, bf16[704,2048]{1,0:T(8,128)(2,1)}, u32[]{:S(2)}) copy-start(bf16[704,2048]{1,0:T(8,128)(2,1)} %param.22) | copy-start | bytes 8650756
  7.2 1.6 copy-start.38
  7.2 2.3 copy-start.36
  7.2 12.8 %copy-start.5 = (bf16[128,2048]{1,0:T(8,128)(2,1)S(1)}, bf16[128,2048]{1,0:T(8,128)(2,1)}, u32[]{:S(2)}) copy-start(bf16[128,2048]{1,0:T(8,128)(2,1)} %param.15) | copy-start | bytes 1572868
  7.2 14.6 %copy-start.30 = (f32[2,2048]{1,0:T(2,128)S(1)}, f32[2,2048]{1,0:T(2,128)}, u32[]{:S(2)}) copy-start(f32[2,2048]{1,0:T(2,128)} %param.16) | copy-start | bytes 49156
  7.2 14.6 %copy-start.31 = (f32[2,2048]{1,0:T(2,128)S(1)}, f32[2,2048]{1,0:T(2,128)}, u32[]{:S(2)}) copy-start(f32[2,2048]{1,0:T(2,128)} %param.17) | copy-start | bytes 49156
  7.3 135.7 %all-gather.5.cloned.1.call-start = ((), (), s32[]{:S(2)}) async-start(), calls=%async_computation.9 | async-start | bytes 28311552 | tf_op jit(solution)/shard_map/all_gather | solution.py:186
  8.0 239.8 %all-gather.7.cloned.1.call-start = ((), (), s32[]{:S(2)}) async-start(), calls=%async_computation.10 | async-start | bytes 9437184 | tf_op jit(solution)/shard_map/all_gather | solution.py:188
  20.2 136.2 %copy-start.32 = (f32[128]{0:T(128)}, f32[128]{0:T(128)S(1)}, u32[]{:S(2)}) copy-start(f32[128]{0:T(128)S(1)} %broadcast_multiply_fusion.6) | copy-start | bytes 1540
  20.5 135.9 %copy-start.34 = (f32[128]{0:T(128)}, f32[128]{0:T(128)S(1)}, u32[]{:S(2)}) copy-start(f32[128]{0:T(128)S(1)} %add_rsqrt_fusion.1) | copy-start | bytes 1540
  21.9 141.2 %copy-start.25 = (f32[128,8]{0,1:T(8,128)}, f32[128,8]{0,1:T(8,128)S(1)}, u32[]{:S(2)}) copy-start(f32[128,8]{0,1:T(8,128)S(1)} %get-tuple-element.253) | copy-start | bytes 12292
  21.9 134.5 %copy-start.21 = (f32[1,2048]{1,0:T(1,128)}, f32[1,2048]{1,0:T(1,128)S(1)}, u32[]{:S(2)}) copy-start(f32[1,2048]{1,0:T(1,128)S(1)} %get-tuple-element.244) | copy-start | bytes 24580
  21.9 134.4 %copy-start.23 = (f32[1,2048]{1,0:T(1,128)}, f32[1,2048]{1,0:T(1,128)S(1)}, u32[]{:S(2)}) copy-start(f32[1,2048]{1,0:T(1,128)S(1)} %get-tuple-element.246) | copy-start | bytes 24580
  164.7 40.2 %all-to-all-start = ((bf16[128,3,8,256]{0,3,1,2:T(8,128)(2,1)}), bf16[128,3,8,256]{0,3,1,2:T(8,128)(2,1)}, u32[]{:S(2)}, u32[]{:S(2)}) async-start(bf16[128,3,8,256]{0,3,1,2:T(8,128)(2,1)} %copy.91), calls=%async_computation | async-start | bytes 3145728 | tf_op jit(solution)/shard_map/all_to_all | solution.py:202
  220.1 2.4 copy-start.7
  220.1 2.4 copy-start.16
  230.9 2.4 copy-start.7
  230.9 2.4 copy-start.16
  243.5 13.9 %all-to-all-start.1 = ((bf16[8,128,256]{1,2,0:T(8,128)(2,1)}), bf16[8,128,256]{1,2,0:T(8,128)(2,1)}, u32[]{:S(2)}, u32[]{:S(2)}) async-start(bf16[8,128,256]{1,2,0:T(8,128)(2,1)} %copy.94), calls=%async_computation.1 | async-start | bytes 1048576 | tf_op jit(solution)/shard_map/all_to_all | solution.py:212
  247.7 52.7 %all-gather.9.cloned.1.call-start = ((), (), s32[]{:S(2)}) async-start(), calls=%async_computation.11 | async-start | bytes 4718592 | tf_op jit(solution)/shard_map/all_gather | solution.py:144
  264.4 75.0 %all-gather.11.cloned.1.call-start = ((), (), s32[]{:S(2)}) async-start(), calls=%async_computation.13 | async-start | bytes 4718592 | tf_op jit(solution)/shard_map/all_gather | solution.py:144
  266.5 145.4 %reduce-scatter.10.cloned.1.call-start = ((), (), s32[]{:S(2)}) async-start(), calls=%async_computation.14 | async-start | bytes 4718592 | tf_op jit(solution)/shard_map/reduce_scatter | solution.py:148
  347.8 1.6 copy-start.40
  360.4 107.0 %reduce-scatter.8.cloned.1.call-start = ((), (), s32[]{:S(2)}) async-start(), calls=%async_computation.12 | async-start | bytes 4718592 | tf_op jit(solution)/shard_map/reduce_scatter | solution.py:148
  366.8 45.0 %copy-start.4 = (f32[128,2048]{1,0:T(8,128)S(1)}, f32[128,2048]{1,0:T(8,128)}, u32[]{:S(2)}) copy-start(f32[128,2048]{1,0:T(8,128)} %copy-done.3) | copy-start | bytes 3145732
  366.8 100.5 %copy-start.18 = (bf16[128,2048]{1,0:T(8,128)(2,1)S(1)}, bf16[128,2048]{1,0:T(8,128)(2,1)}, u32[]{:S(2)}) copy-start(bf16[128,2048]{1,0:T(8,128)(2,1)} %param.25) | copy-start | bytes 1572868
  366.9 245.1 %reduce-scatter.14.cloned.1.call-start = ((), (), s32[]{:S(2)}) async-start(), calls=%async_computation.16 | async-start | bytes 9437184 | tf_op jit(solution)/shard_map/reduce_scatter | solution.py:282
  469.7 7.2 copy-start.9
  483.1 18.0 %copy-start.2 = (bf16[1024,4,64]{0,2,1:T(8,128)(2,1)S(1)}, bf16[1024,4,64]{0,2,1:T(8,128)(2,1)}, u32[]{:S(2)}) copy-start(bf16[1024,4,64]{0,2,1:T(8,128)(2,1)} %get-tuple-element.490) | copy-start | bytes 1572868
  483.1 18.0 %copy-start.8 = (bf16[1024,4,64]{0,2,1:T(8,128)(2,1)S(1)}, bf16[1024,4,64]{0,2,1:T(8,128)(2,1)}, u32[]{:S(2)}) copy-start(bf16[1024,4,64]{0,2,1:T(8,128)(2,1)} %get-tuple-element.491) | copy-start | bytes 1572868
  484.0 13.2 %all-to-all-start.2 = ((bf16[128,8,256]{2,0,1:T(8,128)(2,1)}), bf16[128,8,256]{2,0,1:T(8,128)(2,1)S(1)}, u32[]{:S(2)}, u32[]{:S(2)}) async-start(bf16[128,8,256]{2,0,1:T(8,128)(2,1)} %bitcast.142), calls=%async_computation.4 | async-start | bytes 1048576 | tf_op jit(solution)/shard_map/all_to_all | solution.py:255
  487.5 259.2 %reduce-scatter.12.cloned.1.call-start = ((), (), s32[]{:S(2)}) async-start(), calls=%async_computation.15 | async-start | bytes 28311552 | tf_op jit(solution)/shard_map/reduce_scatter | solution.py:276
  508.9 3.2 copy-start.20
  512.1 2.4 copy-start.14
  524.7 3.2 copy-start.20
  527.9 2.4 copy-start.14
  575.4 2.1 copy-start.26
  575.4 2.1 copy-start.29
  590.5 213.5 %reduce-scatter.16.cloned.1.call-start = ((), (), s32[]{:S(2)}) async-start(), calls=%async_computation.17 | async-start | bytes 589824
  602.8 622.3 %all-reduce.4.cloned.1.call-start = ((), (), s32[]{:S(2)}) async-start(), calls=%async_computation.18 | async-start | bytes 25690112 | tf_op jit(solution)/shard_map/psum | solution.py:289
  746.7 14.7 %copy-start.28 = (f32[2048]{0:T(1024)S(1)}, f32[2048]{0:T(1024)}, u32[]{:S(2)}) copy-start(f32[2048]{0:T(1024)} %get-tuple-element.165) | copy-start | bytes 24580
  746.7 14.7 %copy-start.27 = (f32[2048]{0:T(1024)S(1)}, f32[2048]{0:T(1024)}, u32[]{:S(2)}) copy-start(f32[2048]{0:T(1024)} %get-tuple-element.170) | copy-start | bytes 24580
  746.7 54.9 %copy-start.10 = (f32[128,2048]{1,0:T(8,128)S(1)}, f32[128,2048]{1,0:T(8,128)}, u32[]{:S(2)}) copy-start(f32[128,2048]{1,0:T(8,128)} %copy-done.9) | copy-start | bytes 3145732
  1225.0 2.9 copy-start.12
  1225.0 10.0 slice-start
  1228.0 3.7 copy-start.13
  1228.0 7.1 slice-start.1
  1235.0 6.0 copy-start.1
  (16 other events, 17.8 us)
Sparse Core Ops, SparseCore 0:
  10.0 132.9 all-gather.4
  144.9 68.7 all-gather.6
  264.5 35.7 all-gather.8
  302.7 36.7 all-gather.10
  360.5 51.3 reduce-scatter.9
  416.0 51.2 reduce-scatter.7
  476.9 71.4 reduce-scatter.13
  590.6 155.9 reduce-scatter.11
  750.0 34.2 reduce-scatter.15
  788.2 436.8 all-reduce.3
where the time goes:
time: 1250 us
  waiting for transfers between devices  879 us (70%)
  matrix products  145 us (12%)
  blocking collectives  92.4 us (7%)
  local copies, waits for them, and re-layouts  49.7 us (4%)
  other arithmetic  47.1 us (4%)
  between operations  15.2 us (1%)
  starting transfers between devices  13.4 us (1%)
    psum x1, waiting for transfers between devices, on_device(): lax.psum(mix_shard.astype(jnp.bfloat16), 'grp').astype(jnp.float32)  407 us
    reduce_scatter x1, waiting for transfers between devices, on_device(): lax.psum_scatter(mix_term.astype(jnp.bfloat16), 'seq', scatter_dimension=...  135 us
    all_gather x1, waiting for transfers between devices, on_device(): lax.all_gather(mix_weight, 'seq', axis=2, tiled=True)  121 us
    reduce_scatter x2, waiting for transfers between devices, summed_rows(): lax.psum_scatter(product(left).astype(jnp.bfloat16), 'seq', scatter_dimen...  98.3 us
    all_gather x2, waiting for transfers between devices, gather_rows(): return lax.all_gather(values, 'seq', axis=0, tiled=True)  61.5 us
    psum x1, blocking collectives, on_device(): lax.psum((jnp.stack([gain_one, gain_two]), jnp.stack([bias_one, bias_two]...  40.2 us
    all_to_all x1, waiting for transfers between devices, on_device(): lax.all_to_all(sending.reshape(slots_dev, 3, seq_count, local_width), 'se...  35.6 us
    all_to_all x1, blocking collectives, on_device(): lax.all_to_all(lowered, 'seq', split_axis=0, concat_axis=2, tiled=True)  29.5 us
  transfers between devices with their start and end apart: 13, of which 10 were waited for; matrix products, arithmetic and copies ran while one was open for 15% of the time, Pallas kernels for 0%

commit v1 on v0

--- a/solution.py
+++ b/solution.py
@@ -9,6 +9,27 @@
 EPS = 1e-05
 NEG = -1e30
 BASE = 10000.0
+
+
+def collect(x, axis, dim):
+    size, position, rows = (lax.axis_size(axis), lax.axis_index(axis), x.shape[dim])
+    ahead = [(i, (i + 1) % size) for i in range(size)]
+    backward = [(i, (i - 1) % size) for i in range(size)]
+    whole = jnp.zeros((*x.shape[:dim], size * rows, *x.shape[dim + 1 :]), x.dtype)
+    whole = lax.dynamic_update_slice_in_dim(whole, x, position * rows, axis=dim)
+    from_left = from_right = x
+    halfway = size // 2
+    for lap in range(1, halfway + 1):
+        from_left = lax.ppermute(from_left, axis, ahead)
+        whole = lax.dynamic_update_slice_in_dim(
+            whole, from_left, (position - lap) % size * rows, axis=dim
+        )
+        if lap < size - halfway:
+            from_right = lax.ppermute(from_right, axis, backward)
+            whole = lax.dynamic_update_slice_in_dim(
+                whole, from_right, (position + lap) % size * rows, axis=dim
+            )
+    return whole
 
 
 def layer_norm(values, gain, bias):
@@ -141,7 +162,7 @@
 
 
 def gather_rows(values):
-    return lax.all_gather(values, "seq", axis=0, tiled=True)
+    return collect(values, "seq", 0)
 
 
 def summed_rows(product, left):

time: 1250 us -> 1260 us (level)
  local copies, waits for them, and re-layouts: 49.7 us -> 66.2 us
  starting transfers between devices: 13.4 us -> 29.6 us
  waiting for transfers between devices: 879 us -> 864 us
    ppermute x0 -> x14, waiting for transfers between devices: none -> 84.8 us  [the longest x8 50.1 us: collect(): from_left = lax.ppermute(from_left, axis, ahead)]
    all_gather x2 -> x0, waiting for transfers between devices: 61.5 us -> none  [gather_rows(): return lax.all_gather(values, 'seq', axis=0, tiled=True)]
    all_to_all x1, waiting for transfers between devices: 35.6 us -> 0.01 us  [on_device(): lax.all_to_all(sending.reshape(slots_dev, 3, seq_count, local_width), 'se...]
    ppermute x0 -> x14, starting transfers between devices: none -> 16.3 us  [the longest x6 15.5 us: collect(): from_right = lax.ppermute(from_right, axis, backward)]
  transfers between devices with their start and end apart: 13 -> 25, of which waited for: 10 -> 16; matrix products, arithmetic and copies ran while one was open for 15% -> 15% of each run, Pallas kernels for 0% -> 0%
where the time goes in v1:
time: 1260 us
  waiting for transfers between devices  864 us (69%)
  matrix products  137 us (11%)
  blocking collectives  93.1 us (7%)
  local copies, waits for them, and re-layouts  66.2 us (5%)
  other arithmetic  44 us (3%)
  starting transfers between devices  29.6 us (2%)
  between operations  15.5 us (1%)
    psum x1, waiting for transfers between devices, on_device(): lax.psum(mix_shard.astype(jnp.bfloat16), 'grp').astype(jnp.float32)  407 us
    reduce_scatter x1, waiting for transfers between devices, on_device(): lax.psum_scatter(mix_term.astype(jnp.bfloat16), 'seq', scatter_dimension=...  135 us
    all_gather x1, waiting for transfers between devices, on_device(): lax.all_gather(mix_weight, 'seq', axis=2, tiled=True)  121 us
    reduce_scatter x2, waiting for transfers between devices, summed_rows(): lax.psum_scatter(product(left).astype(jnp.bfloat16), 'seq', scatter_dimen...  100 us
    ppermute x8, waiting for transfers between devices, collect(): from_left = lax.ppermute(from_left, axis, ahead)  50.1 us
    psum x1, blocking collectives, on_device(): lax.psum((jnp.stack([gain_one, gain_two]), jnp.stack([bias_one, bias_two]...  40.2 us
    ppermute x6, waiting for transfers between devices, collect(): from_right = lax.ppermute(from_right, axis, backward)  34.8 us
    all_to_all x1, blocking collectives, on_device(): lax.all_to_all(lowered, 'seq', split_axis=0, concat_axis=2, tiled=True)  30.7 us
  transfers between devices with their start and end apart: 25, of which 16 were waited for; matrix products, arithmetic and copies ran while one was open for 15% of the time, Pallas kernels for 0%

profile of v1, /device:TPU:0, one launch (start us, length us, event | category | flops | bytes accessed | tf_op | source)
XLA Modules:
  0.0 1256.1 jit_solution(14406550334248508599)
XLA Ops:
  9.5 10.4 all_gather.10
  21.9 121.0 %all-gather.3.cloned.1.call-done = bf16[2048,3,2048]{2,0,1:T(8,128)(2,1)} async-done(((bf16[2048,3,256]{2,0,1:T(8,128)(2,1)}), bf16[2048,3,2048]{2,0,1:T(8,128)(2,1)}) %all-gather.3.cloned.1.call-update) | async-done | bytes 25165840 | tf_op jit(solution)/shard_map/all_gather | solution.py:207
  143.0 13.4 %convolution_add_fusion = f32[128,3,2048]{2,0,1:T(8,128)} fusion(bf16[2048,3,2048]{2,0,1:T(8,128)(2,1)} %all-gather.3.cloned.1.call-done, f32[3,2048]{1,0:T(4,128)S(1)} %convert_element_type.139, bf16[128,2048]{1,0:T(8,128)(2,1)S(1)} %copy-done.5, f32[2048]{0:T(1024)S(1)} %bitcast.195, f32[2048]{0:T(1024)S(1)} %bitcast.191, f32[128]{0:T(128)S(1)} %add_rsqrt_fusion.1, ...), kind=kOutput, calls=%fused_computation.63 | convolution fusion | flops 3223584768 | bytes 28877824 | tf_op jit(solution)/shard_map/td,dcf->tcf/dot_general | solution.py:211
  156.4 3.5 copy.90
  164.7 4.4 all-to-all-start
  175.5 47.8 %collective-permute-done.7 = bf16[128,2048]{1,0:T(8,128)(2,1)} collective-permute-done((bf16[128,2048]{1,0:T(8,128)(2,1)}, bf16[128,2048]{1,0:T(8,128)(2,1)}, u32[]{:S(2)}, u32[]{:S(2)}) %collective-permute-start.7) | collective-permute-done | bytes 524320 | tf_op jit(solution)/shard_map/ppermute | solution.py:23
  223.6 3.6 copy.92
  227.1 3.7 reshape.381
  234.1 21.5 %while.27 = (s32[]{:T(128)}, bf16[2,512,4,64]{1,3,2,0:T(8,128)(2,1)}, f32[2,4,512]{2,1,0:T(4,128)S(1)}, s32[2]{0:T(128)S(1)}, s32[1024]{0:T(1024)S(1)}, /*index=...) while((s32[]{:T(128)}, ...), condition=%wide.region_10.11_spmd, body=%wide.region_7.10_spmd.sunk | while | flops 563608064 | bytes 35469596 | solution.py:110
  241.1 3.0 fusion.129
  251.8 3.0 fusion.129
  262.1 4.1 all-to-all-start.1
  270.9 5.5 all-to-all-done.1
  276.5 4.9 fusion.82
  289.1 2.6 collective-permute-start.1
  296.2 3.4 collective-permute-done.12
  300.4 10.3 collective-permute-done.1
  310.7 2.8 collective-permute-start.3
  315.3 9.7 collective-permute-done.3
  325.0 2.8 collective-permute-start.5
  328.5 11.4 collective-permute-done.5
  342.5 6.3 fusion.39
  348.8 7.5 fusion.45
  358.0 8.6 bitcast_convert_fusion
  367.1 6.4 convolution_convert_fusion.3
  373.5 46.7 %reduce-scatter.10.cloned.1.call-done = bf16[128,2048]{1,0:T(8,128)(2,1)} async-done(((bf16[1024,2048]{1,0:T(8,128)(2,1)}), bf16[128,2048]{1,0:T(8,128)(2,1)}) %reduce-scatter.10.cloned.1.call-update) | async-done | bytes 524304 | tf_op jit(solution)/shard_map/reduce_scatter | solution.py:169
  422.4 53.4 %reduce-scatter.8.cloned.1.call-done = bf16[128,2048]{1,0:T(8,128)(2,1)} async-done(((bf16[1024,2048]{1,0:T(8,128)(2,1)}), bf16[128,2048]{1,0:T(8,128)(2,1)}) %reduce-scatter.8.cloned.1.call-update) | async-done | bytes 524304 | tf_op jit(solution)/shard_map/reduce_scatter | solution.py:169
  478.1 7.1 convolution_convert_fusion.1
  485.3 6.3 convolution_convert_fusion.5
  492.4 3.5 all-to-all-start.2
  496.1 9.4 all-to-all-done.2
  509.6 31.6 %while.28 = (s32[]{:T(128)}, f32[1024,4,64]{0,2,1:T(8,128)S(1)}, f32[1024,4,64]{0,2,1:T(8,128)}, bf16[2,512,4,64]{1,3,2,0:T(8,128)(2,1)}, s32[2]{0:T(128)S(1)}, ...) while((s32[]{:T(128)}, f32[1024,4,64]{0,2,1:T(8,128)S(1)}, ...), condition=%wide.region_19.20_spmd.clone, body=%wide.region_17.19_spmd.clone.sunk | while | flops 1376647680 | bytes 87103920 | solution.py:145
  517.3 3.2 multiply_reduce_fusion.4
  533.2 3.2 multiply_reduce_fusion.4
  544.9 2.9 copy.98
  547.8 30.7 %all_to_all.56 = bf16[1024,3,1,256]{3,1,2,0:T(4,128)(2,1)S(1)} all-to-all(bf16[1024,3,1,256]{3,1,2,0:T(4,128)(2,1)S(1)} %copy.98), channel_id=1, replica_groups=mesh['grp'=4,'seq'=8] {'seq'}, dimensions={0} | all-to-all | bytes 3145728 | tf_op jit(solution)/shard_map/all_to_all | solution.py:287
  586.8 11.9 convolution_convert_fusion
  598.8 10.8 convolution_convert_fusion.2
  611.3 8.9 convolution_convert_fusion.4
  620.1 134.7 %reduce-scatter.12.cloned.1.call-done = bf16[2048,3,256]{2,0,1:T(8,128)(2,1)} async-done(((bf16[2048,3,2048]{2,0,1:T(8,128)(2,1)}), bf16[2048,3,256]{2,0,1:T(8,128)(2,1)}) %reduce-scatter.12.cloned.1.call-update) | async-done | bytes 3145744 | tf_op jit(solution)/shard_map/reduce_scatter | solution.py:297
  754.9 14.6 %fusion.59 = (f32[2048]{0:T(1024)S(1)}, f32[128]{0:T(128)S(1)}, f32[128]{0:T(128)S(1)}, f32[2048]{0:T(1024)S(1)}, f32[128,2048]{1,0:T(8,128)}) fusion(bf16[128,2048]{1,0:T(8,128)(2,1)S(1)} %copy-done.6, f32[128]{0:T(128)S(1)} %copy-done.40, f32[128]{0:T(128)S(1)} %copy-done.38, f32[2048]{0:T(1024)S(1)} %bitcast.193, ...), kind=kOutput, calls=%fused_computation.93 | convolution fusion | flops 3225415680 | bytes 28338176 | tf_op jit(solution)/shard_map/tcf,dcf->td/dot_general | solution.py:293
  769.6 40.2 %all-reduce = (f32[2,2048]{1,0:T(2,128)}, f32[2,2048]{1,0:T(2,128)}) all-reduce(f32[2,2048]{1,0:T(2,128)S(1)} %pad_maximum_fusion.10, f32[2,2048]{1,0:T(2,128)S(1)} %pad_maximum_fusion.11), channel_id=1, replica_groups=mesh['grp'=4,'seq'=8] {'grp','seq'}, use_global_device_ids=true, to_apply=%region_24.25 | all-reduce | flops 8192 | bytes 65536 | tf_op jit(solution)/shard_map/psum | solution.py:316
  813.2 11.9 psum.52
  825.7 407.2 %all-reduce.4.cloned.1.call-done = (bf16[2048,3,256]{2,0,1:T(8,128)(2,1)}, bf16[256,2048]{1,0:T(8,128)(2,1)}, bf16[2048,2,704]{0,2,1:T(8,128)(2,1)}, bf16[704,2048]{1,0:T(8,128)(2,1)}) async-done(((bf16[2048,3,256]{2,0,1:T(8,128)(2,1)}, bf16[256,2048]{1,0:T(8,128)(2,1)}, bf16[2048,2,704]{0,2,1:T(8,128)(2,1)}, bf16[704,2048]{1,0:T(8,128)(2,1)}), (bf16[2048,3,256]{2,0,1:T(8,128)(2,1)}, ...) | async-done | bytes 12845072 | tf_op jit(solution)/shard_map/psum | solution.py:310
  1232.9 2.9 convert_element_type.164
  1235.8 3.7 convert_element_type.161
  1239.5 3.3 convert_element_type.168
  1242.9 6.0 convert_element_type.166
  (285 shorter events, 111.2 us)
Async XLA Ops:
  7.2 341.6 %copy-start = (bf16[704,2048]{1,0:T(8,128)(2,1)S(1)}, bf16[704,2048]{1,0:T(8,128)(2,1)}, u32[]{:S(2)}) copy-start(bf16[704,2048]{1,0:T(8,128)(2,1)} %param.22) | copy-start | bytes 8650756
  7.2 12.8 %copy-start.5 = (bf16[128,2048]{1,0:T(8,128)(2,1)S(1)}, bf16[128,2048]{1,0:T(8,128)(2,1)}, u32[]{:S(2)}) copy-start(bf16[128,2048]{1,0:T(8,128)(2,1)} %param.15) | copy-start | bytes 1572868
  7.2 14.6 %copy-start.35 = (f32[2,2048]{1,0:T(2,128)S(1)}, f32[2,2048]{1,0:T(2,128)}, u32[]{:S(2)}) copy-start(f32[2,2048]{1,0:T(2,128)} %param.16) | copy-start | bytes 49156
  7.2 14.6 %copy-start.36 = (f32[2,2048]{1,0:T(2,128)S(1)}, f32[2,2048]{1,0:T(2,128)}, u32[]{:S(2)}) copy-start(f32[2,2048]{1,0:T(2,128)} %param.17) | copy-start | bytes 49156
  7.3 135.7 %all-gather.3.cloned.1.call-start = ((), (), s32[]{:S(2)}) async-start(), calls=%async_computation.9 | async-start | bytes 28311552 | tf_op jit(solution)/shard_map/all_gather | solution.py:207
  8.0 262.9 %all-gather.5.cloned.1.call-start = ((), (), s32[]{:S(2)}) async-start(), calls=%async_computation.10 | async-start | bytes 9437184 | tf_op jit(solution)/shard_map/all_gather | solution.py:209
  20.2 136.2 %copy-start.37 = (f32[128]{0:T(128)}, f32[128]{0:T(128)S(1)}, u32[]{:S(2)}) copy-start(f32[128]{0:T(128)S(1)} %broadcast_multiply_fusion.6) | copy-start | bytes 1540
  20.5 135.9 %copy-start.39 = (f32[128]{0:T(128)}, f32[128]{0:T(128)S(1)}, u32[]{:S(2)}) copy-start(f32[128]{0:T(128)S(1)} %add_rsqrt_fusion.1) | copy-start | bytes 1540
  21.9 141.2 %copy-start.30 = (f32[128,8]{0,1:T(8,128)}, f32[128,8]{0,1:T(8,128)S(1)}, u32[]{:S(2)}) copy-start(f32[128,8]{0,1:T(8,128)S(1)} %get-tuple-element.257) | copy-start | bytes 12292
  21.9 134.5 %copy-start.26 = (f32[1,2048]{1,0:T(1,128)}, f32[1,2048]{1,0:T(1,128)S(1)}, u32[]{:S(2)}) copy-start(f32[1,2048]{1,0:T(1,128)S(1)} %get-tuple-element.248) | copy-start | bytes 24580
  21.9 134.4 %copy-start.28 = (f32[1,2048]{1,0:T(1,128)}, f32[1,2048]{1,0:T(1,128)S(1)}, u32[]{:S(2)}) copy-start(f32[1,2048]{1,0:T(1,128)S(1)} %get-tuple-element.250) | copy-start | bytes 24580
  164.7 7.0 copy-start.21
  164.7 58.9 %all-to-all-start = ((bf16[128,3,8,256]{0,3,1,2:T(8,128)(2,1)}), bf16[128,3,8,256]{0,3,1,2:T(8,128)(2,1)}, u32[]{:S(2)}, u32[]{:S(2)}) async-start(bf16[128,3,8,256]{0,3,1,2:T(8,128)(2,1)} %copy.91), calls=%async_computation | async-start | bytes 3145728 | tf_op jit(solution)/shard_map/all_to_all | solution.py:223
  172.8 50.5 %collective-permute-start.7 = (bf16[128,2048]{1,0:T(8,128)(2,1)}, bf16[128,2048]{1,0:T(8,128)(2,1)}, u32[]{:S(2)}, u32[]{:S(2)}) collective-permute-start(bf16[128,2048]{1,0:T(8,128)(2,1)} %get-tuple-element.218), channel_id=1, source_target_pairs={{0,1},{1,2},{2,3},{3,4},{4,5},{5,6},{6,7},{7,0},{8,9},{9,10},{10,1... | collective-permute-start | bytes 1572872 | tf_op jit(solution)/shard_map/ppermute | solution.py:23
  173.2 93.2 %collective-permute-start.8 = (bf16[128,2048]{1,0:T(8,128)(2,1)}, bf16[128,2048]{1,0:T(8,128)(2,1)}, u32[]{:S(2)}, u32[]{:S(2)}) collective-permute-start(bf16[128,2048]{1,0:T(8,128)(2,1)} %get-tuple-element.218), channel_id=1, source_target_pairs={{0,7},{1,0},{2,1},{3,2},{4,3},{5,4},{6,5},{7,6},{8,15},{9,8},{10,9... | collective-permute-start | bytes 1572872 | tf_op jit(solution)/shard_map/ppermute | solution.py:28
  223.3 47.6 %collective-permute-start.9 = (bf16[128,2048]{1,0:T(8,128)(2,1)}, bf16[128,2048]{1,0:T(8,128)(2,1)}, u32[]{:S(2)}, u32[]{:S(2)}) collective-permute-start(bf16[128,2048]{1,0:T(8,128)(2,1)} %collective-permute-done.7), channel_id=1, source_target_pairs={{0,1},{1,2},{2,3},{3,4},{4,5},{5,6},{6,7},{7,0},{8,9},{9,10},{10,1... | collective-permute-start | bytes 1572872 | tf_op jit(solution)/shard_map/ppermute | solution.py:23
  262.1 14.4 %all-to-all-start.1 = ((bf16[8,128,256]{1,2,0:T(8,128)(2,1)}), bf16[8,128,256]{1,2,0:T(8,128)(2,1)}, u32[]{:S(2)}, u32[]{:S(2)}) async-start(bf16[8,128,256]{1,2,0:T(8,128)(2,1)} %copy.94), calls=%async_computation.1 | async-start | bytes 1048576 | tf_op jit(solution)/shard_map/all_to_all | solution.py:233
  266.2 154.0 %reduce-scatter.10.cloned.1.call-start = ((), (), s32[]{:S(2)}) async-start(), calls=%async_computation.12 | async-start | bytes 4718592 | tf_op jit(solution)/shard_map/reduce_scatter | solution.py:169
  266.4 18.5 %collective-permute-start.10 = (bf16[128,2048]{1,0:T(8,128)(2,1)}, bf16[128,2048]{1,0:T(8,128)(2,1)}, u32[]{:S(2)}, u32[]{:S(2)}) collective-permute-start(bf16[128,2048]{1,0:T(8,128)(2,1)} %collective-permute-done.8), channel_id=1, source_target_pairs={{0,7},{1,0},{2,1},{3,2},{4,3},{5,4},{6,5},{7,6},{8,15},{9,8},{10,9... | collective-permute-start | bytes 1572872 | tf_op jit(solution)/shard_map/ppermute | solution.py:28
  270.9 18.2 %collective-permute-start.11 = (bf16[128,2048]{1,0:T(8,128)(2,1)}, bf16[128,2048]{1,0:T(8,128)(2,1)}, u32[]{:S(2)}, u32[]{:S(2)}) collective-permute-start(bf16[128,2048]{1,0:T(8,128)(2,1)} %collective-permute-done.9), channel_id=1, source_target_pairs={{0,1},{1,2},{2,3},{3,4},{4,5},{5,6},{6,7},{7,0},{8,9},{9,10},{10,1... | collective-permute-start | bytes 1572872 | tf_op jit(solution)/shard_map/ppermute | solution.py:23
  281.7 60.8 %slice-start.2 = ((s8[5767168]{0:T(1024)(128)(4,1)}), s8[4194304]{0:T(1024)(128)(4,1)S(1)}, s32[]{:S(2)}) async-start(s8[5767168]{0:T(1024)(128)(4,1)} %bitcast.206), calls=%async_computation.19 | async-start | bytes 8388608
  282.5 11.8 collective-permute-start
  284.9 14.7 %collective-permute-start.12 = (bf16[128,2048]{1,0:T(8,128)(2,1)}, bf16[128,2048]{1,0:T(8,128)(2,1)S(1)}, u32[]{:S(2)}, u32[]{:S(2)}) collective-permute-start(bf16[128,2048]{1,0:T(8,128)(2,1)} %collective-permute-done.10), channel_id=1, source_target_pairs={{0,7},{1,0},{2,1},{3,2},{4,3},{5,4},{6,5},{7,6},{8,15},{9,8},{10,9... | collective-permute-start | bytes 1572872 | tf_op jit(solution)/shard_map/ppermute | solution.py:28
  289.1 24.4 %collective-permute-start.13 = (bf16[128,2048]{1,0:T(8,128)(2,1)}, bf16[128,2048]{1,0:T(8,128)(2,1)S(1)}, u32[]{:S(2)}, u32[]{:S(2)}) collective-permute-start(bf16[128,2048]{1,0:T(8,128)(2,1)} %collective-permute-done.11), channel_id=1, source_target_pairs={{0,1},{1,2},{2,3},{3,4},{4,5},{5,6},{6,7},{7,0},{8,9},{9,10},{10,1... | collective-permute-start | bytes 1572872 | tf_op jit(solution)/shard_map/ppermute | solution.py:23
  289.1 21.6 %collective-permute-start.1 = (bf16[128,2048]{1,0:T(8,128)(2,1)S(1)}, bf16[128,2048]{1,0:T(8,128)(2,1)S(1)}, u32[]{:S(2)}, u32[]{:S(2)}) collective-permute-start(bf16[128,2048]{1,0:T(8,128)(2,1)S(1)} %get-tuple-element.220), channel_id=1, source_target_pairs={{0,7},{1,0},{2,1},{3,2},{4,3},{5,4},{6,5},{7,6},{8,15},{9,8},{10,9... | collective-permute-start | bytes 1572872 | tf_op jit(solution)/shard_map/ppermute | solution.py:28
  293.6 48.9 %slice-start.3 = ((s8[5767168]{0:T(1024)(128)(4,1)}), s8[1572864]{0:T(1024)(128)(4,1)S(1)}, s32[]{:S(2)}) async-start(s8[5767168]{0:T(1024)(128)(4,1)} %bitcast.206), calls=%async_computation.20 | async-start | bytes 3145728
  294.3 20.9 %collective-permute-start.2 = (bf16[128,2048]{1,0:T(8,128)(2,1)S(1)}, bf16[128,2048]{1,0:T(8,128)(2,1)S(1)}, u32[]{:S(2)}, u32[]{:S(2)}) collective-permute-start(bf16[128,2048]{1,0:T(8,128)(2,1)S(1)} %collective-permute-done), channel_id=1, source_target_pairs={{0,1},{1,2},{2,3},{3,4},{4,5},{5,6},{6,7},{7,0},{8,9},{9,10},{10,1... | collective-permute-start | bytes 1572872 | tf_op jit(solution)/shard_map/ppermute | solution.py:23
  310.7 14.3 %collective-permute-start.3 = (bf16[128,2048]{1,0:T(8,128)(2,1)S(1)}, bf16[128,2048]{1,0:T(8,128)(2,1)S(1)}, u32[]{:S(2)}, u32[]{:S(2)}) collective-permute-start(bf16[128,2048]{1,0:T(8,128)(2,1)S(1)} %collective-permute-done.1), channel_id=1, source_target_pairs={{0,7},{1,0},{2,1},{3,2},{4,3},{5,4},{6,5},{7,6},{8,15},{9,8},{10,9... | collective-permute-start | bytes 1572872 | tf_op jit(solution)/shard_map/ppermute | solution.py:28
  315.2 12.9 %collective-permute-start.4 = (bf16[128,2048]{1,0:T(8,128)(2,1)S(1)}, bf16[128,2048]{1,0:T(8,128)(2,1)S(1)}, u32[]{:S(2)}, u32[]{:S(2)}) collective-permute-start(bf16[128,2048]{1,0:T(8,128)(2,1)S(1)} %collective-permute-done.2), channel_id=1, source_target_pairs={{0,1},{1,2},{2,3},{3,4},{4,5},{5,6},{6,7},{7,0},{8,9},{9,10},{10,1... | collective-permute-start | bytes 1572872 | tf_op jit(solution)/shard_map/ppermute | solution.py:23
  325.0 14.9 %collective-permute-start.5 = (bf16[128,2048]{1,0:T(8,128)(2,1)S(1)}, bf16[128,2048]{1,0:T(8,128)(2,1)S(1)}, u32[]{:S(2)}, u32[]{:S(2)}) collective-permute-start(bf16[128,2048]{1,0:T(8,128)(2,1)S(1)} %collective-permute-done.3), channel_id=1, source_target_pairs={{0,7},{1,0},{2,1},{3,2},{4,3},{5,4},{6,5},{7,6},{8,15},{9,8},{10,9... | collective-permute-start | bytes 1572872 | tf_op jit(solution)/shard_map/ppermute | solution.py:28
  328.1 12.3 collective-permute-start.6
  366.5 109.2 %reduce-scatter.8.cloned.1.call-start = ((), (), s32[]{:S(2)}) async-start(), calls=%async_computation.11 | async-start | bytes 4718592 | tf_op jit(solution)/shard_map/reduce_scatter | solution.py:169
  373.5 46.8 %copy-start.4 = (f32[128,2048]{1,0:T(8,128)S(1)}, f32[128,2048]{1,0:T(8,128)}, u32[]{:S(2)}) copy-start(f32[128,2048]{1,0:T(8,128)} %copy-done.3) | copy-start | bytes 3145732
  373.5 102.3 %copy-start.22 = (bf16[128,2048]{1,0:T(8,128)(2,1)S(1)}, bf16[128,2048]{1,0:T(8,128)(2,1)}, u32[]{:S(2)}) copy-start(bf16[128,2048]{1,0:T(8,128)(2,1)} %param.25) | copy-start | bytes 1572868
  373.5 246.7 %reduce-scatter.14.cloned.1.call-start = ((), (), s32[]{:S(2)}) async-start(), calls=%async_computation.14 | async-start | bytes 9437184 | tf_op jit(solution)/shard_map/reduce_scatter | solution.py:303
  478.1 7.2 copy-start.9
  491.5 18.0 %copy-start.2 = (bf16[1024,4,64]{0,2,1:T(8,128)(2,1)S(1)}, bf16[1024,4,64]{0,2,1:T(8,128)(2,1)}, u32[]{:S(2)}) copy-start(bf16[1024,4,64]{0,2,1:T(8,128)(2,1)} %get-tuple-element.492) | copy-start | bytes 1572868
  491.6 18.0 %copy-start.8 = (bf16[1024,4,64]{0,2,1:T(8,128)(2,1)S(1)}, bf16[1024,4,64]{0,2,1:T(8,128)(2,1)}, u32[]{:S(2)}) copy-start(bf16[1024,4,64]{0,2,1:T(8,128)(2,1)} %get-tuple-element.493) | copy-start | bytes 1572868
  492.4 13.2 %all-to-all-start.2 = ((bf16[128,8,256]{2,0,1:T(8,128)(2,1)}), bf16[128,8,256]{2,0,1:T(8,128)(2,1)S(1)}, u32[]{:S(2)}, u32[]{:S(2)}) async-start(bf16[128,8,256]{2,0,1:T(8,128)(2,1)} %bitcast.142), calls=%async_computation.4 | async-start | bytes 1048576 | tf_op jit(solution)/shard_map/all_to_all | solution.py:276
  495.9 259.0 %reduce-scatter.12.cloned.1.call-start = ((), (), s32[]{:S(2)}) async-start(), calls=%async_computation.13 | async-start | bytes 28311552 | tf_op jit(solution)/shard_map/reduce_scatter | solution.py:297
  598.7 213.5 %reduce-scatter.16.cloned.1.call-start = ((), (), s32[]{:S(2)}) async-start(), calls=%async_computation.15 | async-start | bytes 589824
  611.0 621.9 %all-reduce.4.cloned.1.call-start = ((), (), s32[]{:S(2)}) async-start(), calls=%async_computation.16 | async-start | bytes 25690112 | tf_op jit(solution)/shard_map/psum | solution.py:310
  754.9 14.7 %copy-start.33 = (f32[2048]{0:T(1024)S(1)}, f32[2048]{0:T(1024)}, u32[]{:S(2)}) copy-start(f32[2048]{0:T(1024)} %get-tuple-element.165) | copy-start | bytes 24580
  754.9 14.7 %copy-start.32 = (f32[2048]{0:T(1024)S(1)}, f32[2048]{0:T(1024)}, u32[]{:S(2)}) copy-start(f32[2048]{0:T(1024)} %get-tuple-element.170) | copy-start | bytes 24580
  754.9 54.9 %copy-start.10 = (f32[128,2048]{1,0:T(8,128)S(1)}, f32[128,2048]{1,0:T(8,128)}, u32[]{:S(2)}) copy-start(f32[128,2048]{1,0:T(8,128)} %copy-done.9) | copy-start | bytes 3145732
  1232.9 10.0 slice-start
  1235.8 7.1 slice-start.1
  1242.9 6.0 copy-start.1
  (35 other events, 65.3 us)
Sparse Core Ops, SparseCore 0:
  10.0 132.9 all-gather.2
  144.9 76.6 all-gather.4
  366.7 53.5 reduce-scatter.9
  424.4 51.3 reduce-scatter.7
  485.4 73.0 reduce-scatter.13
  598.9 155.9 reduce-scatter.11
  758.2 34.2 reduce-scatter.15
  796.0 436.8 all-reduce.3
